TPU v7x, 32 devices: a whole 2x2x4 slice. The times are simulated.
32 devices in a mesh: inner: 8 (over y, x, core), outer: 4 (over z).
Axes of the slice: x: 2, y: 2, z: 4, core: 2. Of those that a mesh axis runs over, the one named last changes fastest.
Arguments:
- query_rows: bfloat16 [8, 1024, 1024], P('inner', 'outer'), may hold values from -120 to 120
- key_rows: bfloat16 [8, 1024, 128], P('inner', 'outer'), may hold values from -6 to 6
- value_rows: bfloat16 [8, 1024, 128], P('inner', 'outer'), may hold values from -6 to 6
- out_grad: bfloat16 [8, 1024, 1024], P('inner', 'outer'), may hold values from -6 to 6
- doc_start: int32 [8, 1024], P('inner', 'outer'), may hold values from 0 to 8191, as said below
Outputs:
- query_grad: bfloat16 [8, 1024, 1024], P('inner', 'outer')
- key_grad: bfloat16 [8, 1024, 128], P('inner', 'outer')
- value_grad: bfloat16 [8, 1024, 128], P('inner', 'outer')
Inputs may be any that keep to these rules, and one draw needn't show every extreme that they name: doc_start[p] <= p, doc_start never falls along the sequence, and doc_start[doc_start[p]] = doc_start[p]; the tokens at position 0 and at the last position each start a document.
All inputs are finite; a program needn't handle non-finite values.
Results may differ from a plain program's by a relative error of at most 0.0075.
Values may be sent and summed in bfloat16 or wider, within the bound.
A program may use at most 64 MiB of HBM per device.

v0:
```python
import functools

import jax
import jax.numpy as jnp
from jax import lax
from jax.experimental import pallas as pl
from jax.experimental.pallas import tpu as pltpu
from jax.sharding import PartitionSpec as P

NEG_FILL = -1e30
LOG2E = 1.4426950408889634
VMEM_BYTES = 48 * 1024 * 1024
MESH = pl.DeviceIdType.MESH
HEADS_PER_STEP = 8
GREET = (1, -1, 2, -2)
CONTRACT_LAST = (((1,), (1,)), ((), ()))


def dot_last(left, right):
    return lax.dot_general(left, right, CONTRACT_LAST, preferred_element_type=jnp.float32)


def dot(left, right):
    return jnp.dot(left, right, preferred_element_type=jnp.float32)


def kernel(
    inner_size, outer_size,
    q_ref, k_ref, v_ref, g_ref, start_ref,
    dq_ref, dk_ref, dv_ref,
    qs, gs, ks, vs, kt, bias, early, prob, plow, ds, start_rows, own_sum, part, came,
    local_sem, send_sem, recv_sem,
):
    length = k_ref.shape[1]
    size = k_ref.shape[2]
    heads = q_ref.shape[2] // size
    scale = size ** (-0.5)
    blocks = inner_size * outer_size
    block = lax.axis_index("inner") * outer_size + lax.axis_index("outer")

    def at(step):
        other = lax.rem(block + step + blocks, blocks)
        return (other // outer_size, lax.rem(other, outer_size))

    barrier = pltpu.get_barrier_semaphore()
    for step in GREET:
        pl.semaphore_signal(barrier, inc=1, device_id=at(step), device_id_type=MESH)

    loads = []

    def load(source, target):
        copy = pltpu.make_async_copy(source, target, local_sem.at[len(loads)])
        copy.start()
        loads.append(copy)

    load(start_ref, start_rows)
    load(k_ref.at[0], ks.at[pl.ds(0, length)])
    load(v_ref.at[0], vs.at[pl.ds(0, length)])
    for head in range(heads):
        load(q_ref.at[0, :, pl.ds(head * size, size)], qs.at[pl.ds(head * length, length)])
        load(g_ref.at[0, :, pl.ds(head * size, size)], gs.at[pl.ds(head * length, length)])

    pl.semaphore_wait(barrier, len(GREET))
    sends = []

    def send(source, target, step):
        which = len(sends)
        copy = pltpu.make_async_remote_copy(
            src_ref=source, dst_ref=target,
            send_sem=send_sem.at[which], recv_sem=recv_sem.at[which],
            device_id=at(step), device_id_type=MESH,
        )
        copy.start()
        sends.append(copy)
        return copy

    key_near = send(k_ref.at[0], ks.at[pl.ds(length, length)], 1)
    value_near = send(v_ref.at[0], vs.at[pl.ds(length, length)], 1)

    first = block * length
    key_at = lax.broadcasted_iota(jnp.int32, (length, length), 0)
    query_at = lax.broadcasted_iota(jnp.int32, (length, length), 1)
    causal = key_at <= query_at
    loads[0].wait()
    starts = start_rows[...]
    mixed_pos = first + key_at - jnp.where(causal, 0, 2 * length)
    bias[pl.ds(0, length)] = jnp.where(mixed_pos >= starts, 0.0, NEG_FILL)
    bias[pl.ds(length, length)] = jnp.where(first - length + key_at >= starts, 0.0, NEG_FILL)

    for copy in loads[1:]:
        copy.wait()

    def split(mixed):
        is_own = lax.broadcasted_iota(jnp.int32, (length, length), 0) <= lax.broadcasted_iota(
            jnp.int32, (length, length), 1
        )
        zero = jnp.zeros_like(mixed)
        return (
            jnp.where(is_own, mixed, zero).astype(jnp.bfloat16),
            jnp.where(is_own, zero, mixed).astype(jnp.bfloat16),
        )

    def merge(own, far):
        is_own = lax.broadcasted_iota(jnp.int32, (length, length), 0) <= lax.broadcasted_iota(
            jnp.int32, (length, length), 1
        )
        return jnp.where(is_own, own, far)

    def put(target, head, mixed, near):
        columns = pl.ds(pl.multiple_of(head * length, length), length)
        own, far = split(mixed)
        target[pl.ds(0, length), columns] = own
        target[pl.ds(length, length), columns] = near.astype(jnp.bfloat16)
        target[pl.ds(2 * length, length), columns] = far

    def over_heads(body):
        def step(index, carry):
            for inside in range(HEADS_PER_STEP):
                body(index * HEADS_PER_STEP + inside)
            return carry

        lax.fori_loop(0, heads // HEADS_PER_STEP, step, 0)

    def rows_of(head):
        return pl.ds(pl.multiple_of(head * length, length), length)

    own_rows, near_rows, far_rows = (pl.ds(tile * length, length) for tile in range(3))

    def own_tile(head):
        early[0, head] = dot_last(ks[own_rows], qs[rows_of(head)]) + bias[own_rows]
        early[2, head] = dot_last(vs[own_rows], gs[rows_of(head)])

    def near_scores(head):
        early[1, head] = dot_last(ks[near_rows], qs[rows_of(head)]) + bias[near_rows]

    def near_grads(head):
        early[3, head] = dot_last(vs[near_rows], gs[rows_of(head)])

    over_heads(own_tile)
    key_near.wait_recv()
    key_far = send(ks.at[near_rows], ks.at[far_rows], 1)
    over_heads(near_scores)
    value_near.wait_recv()
    value_far = send(vs.at[near_rows], vs.at[far_rows], 1)
    over_heads(near_grads)
    key_far.wait_recv()

    def forward(head):
        far = dot_last(ks[far_rows], qs[rows_of(head)]) + bias[own_rows]
        mixed = merge(early[0, head], far)
        near = early[1, head]
        top = jnp.maximum(
            jnp.max(mixed, axis=0, keepdims=True), jnp.max(near, axis=0, keepdims=True)
        )
        mixed = jnp.exp2((mixed - top) * (scale * LOG2E))
        near = jnp.exp2((near - top) * (scale * LOG2E))
        total = jnp.sum(mixed, axis=0, keepdims=True) + jnp.sum(near, axis=0, keepdims=True)
        inverse = 1.0 / total
        mixed = mixed * inverse
        near = near * inverse
        prob[head, pl.ds(0, length)] = mixed
        prob[head, pl.ds(length, length)] = near
        put(plow, head, mixed, near)

    over_heads(forward)

    def give_back(weights, rows, kind):
        copies = []
        for tile in (2, 1):
            slot = 2 * kind + tile - 1
            part[slot] = dot(weights[pl.ds(tile * length, length)], rows[...]).astype(jnp.bfloat16)
            copies.append(send(part.at[slot], came.at[slot], -tile))
        return copies

    value_parts = give_back(plow, gs, 0)
    value_far.wait_recv()

    def backward(head):
        mixed = merge(early[2, head], dot_last(vs[far_rows], gs[rows_of(head)]))
        near = early[3, head]
        mixed_prob = prob[head, pl.ds(0, length)]
        near_prob = prob[head, pl.ds(length, length)]
        delta = jnp.sum(mixed_prob * mixed, axis=0, keepdims=True) + jnp.sum(
            near_prob * near, axis=0, keepdims=True
        )
        put(ds, head, mixed_prob * (mixed - delta), near_prob * (near - delta))

    over_heads(backward)
    key_parts = give_back(ds, qs, 1)

    own_sum[0] = dot(plow[own_rows], gs[...])
    own_sum[1] = dot(ds[own_rows], qs[...])
    kt[...] = ks[...].astype(jnp.float32).T.astype(jnp.bfloat16)

    for head in range(heads):
        turned = dot(kt[...], ds[:, pl.ds(head * length, length)]) * scale
        dq_ref[:, pl.ds(head * size, size)] = turned.T.astype(jnp.bfloat16)

    for copy in value_parts:
        copy.wait_recv()
    dv_ref[...] = (
        own_sum[0] + came[0].astype(jnp.float32) + came[1].astype(jnp.float32)
    ).astype(jnp.bfloat16)
    for copy in key_parts:
        copy.wait_recv()
    dk_ref[...] = (
        (own_sum[1] + came[2].astype(jnp.float32) + came[3].astype(jnp.float32)) * scale
    ).astype(jnp.bfloat16)
    for copy in sends:
        copy.wait_send()


def write_out(dq_from, dk_from, dv_from, dq_ref, dk_ref, dv_ref, sem):
    pairs = ((dq_from, dq_ref), (dk_from, dk_ref), (dv_from, dv_ref))
    copies = [
        pltpu.make_async_copy(source, target.at[0], sem.at[which])
        for which, (source, target) in enumerate(pairs)
    ]
    for copy in copies:
        copy.start()
    for copy in copies:
        copy.wait()


def on_device(inner_size, outer_size, query_rows, key_rows, value_rows, out_grad, doc_start):
    length, size = key_rows.shape[1:]
    heads = query_rows.shape[2] // size
    low, wide = jnp.bfloat16, jnp.float32
    far = pl.BlockSpec(memory_space=pltpu.HBM)
    near = pl.BlockSpec(memory_space=pltpu.VMEM)
    given = (query_rows, key_rows, value_rows, out_grad, doc_start)
    results = pl.pallas_call(
        functools.partial(kernel, inner_size, outer_size),
        out_shape=(
            jax.ShapeDtypeStruct(query_rows.shape[1:], low),
            jax.ShapeDtypeStruct(key_rows.shape[1:], low),
            jax.ShapeDtypeStruct(value_rows.shape[1:], low),
        ),
        in_specs=[far] * 5,
        out_specs=(near, near, near),
        scratch_shapes=[
            pltpu.VMEM((heads * length, size), low),
            pltpu.VMEM((heads * length, size), low),
            pltpu.VMEM((3 * length, size), low),
            pltpu.VMEM((3 * length, size), low),
            pltpu.VMEM((size, 3 * length), low),
            pltpu.VMEM((2 * length, length), wide),
            pltpu.VMEM((4, heads, length, length), wide),
            pltpu.VMEM((heads, 2 * length, length), wide),
            pltpu.VMEM((3 * length, heads * length), low),
            pltpu.VMEM((3 * length, heads * length), low),
            pltpu.VMEM((1, length), jnp.int32),
            pltpu.VMEM((2, length, size), wide),
            pltpu.VMEM((4, length, size), low),
            pltpu.VMEM((4, length, size), low),
            pltpu.SemaphoreType.DMA((3 + 2 * heads,)),
            pltpu.SemaphoreType.DMA((8,)),
            pltpu.SemaphoreType.DMA((8,)),
        ],
        compiler_params=pltpu.CompilerParams(
            collective_id=0, has_side_effects=True, vmem_limit_bytes=VMEM_BYTES
        ),
        name="window_attention_grad",
    )(*(pltpu.with_memory_space_constraint(rows, pltpu.HBM) for rows in given))
    return pl.pallas_call(
        write_out,
        out_shape=tuple(jax.ShapeDtypeStruct((1,) + result.shape, low) for result in results),
        in_specs=[near] * 3,
        out_specs=(far,) * 3,
        scratch_shapes=[pltpu.SemaphoreType.DMA((3,))],
        compiler_params=pltpu.CompilerParams(vmem_limit_bytes=1024 * 1024),
        name="write_out",
    )(*results)


def solution(mesh):
    rows = P("inner", "outer", None)
    return jax.shard_map(
        functools.partial(on_device, mesh.shape["inner"], mesh.shape["outer"]),
        mesh=mesh,
        in_specs=(rows, rows, rows, rows, P("inner", "outer")),
        out_specs=(rows, rows, rows),
        check_vma=False,
    )
```

profile of v0, /device:TPU:0, one launch (start us, length us, event | category | flops | bytes accessed | tf_op | source)
XLA Modules:
  0.0 23.7 jit_solution(15556650360130795394)
XLA Ops:
  0.6 22.2 %window_attention_grad.1 = (bf16[256,1024]{1,0:T(8,128)(2,1)S(1)}, bf16[256,128]{1,0:T(8,128)(2,1)S(1)}, bf16[256,128]{1,0:T(8,128)(2,1)S(1)}) custom-call(bf16[1,256,1024]{2,1,0:T(8,128)(2,1)} %q_ref.1, bf16[1,256,128]{2,1,0:T(8,128)(2,1)} %k_ref.1, bf16[1,256,128]{2,1,0:T(8,128)(2,1)} %v_ref.1, bf16[1,256,1024]{2,1,0:T(8,128)(2,1)} %g_ref.1, ...), custom_call_target="tpu_custom_call" | custom-call | tf_op jit(solution)/shard_map/window_attention_grad/pallas_call | solution.py:232
  22.9 0.9 %write_out.1 = (bf16[1,256,1024]{2,1,0:T(8,128)(2,1)}, bf16[1,256,128]{2,1,0:T(8,128)(2,1)}, bf16[1,256,128]{2,1,0:T(8,128)(2,1)}) custom-call(bf16[256,1024]{1,0:T(8,128)(2,1)S(1)} %get-tuple-element.6.dq_from, bf16[256,128]{1,0:T(8,128)(2,1)S(1)} %get-tuple-element.7.dk_from, bf16[256,128]{1,0:T(8,128)(2,1)S(1)} %get-tuple-element.8.dv_from), custom_call_target="tpu_custom_call" | custom-call | tf_op jit(solution)/shard_map/write_out/pallas_call | solution.py:265
where the time goes:
time: 23.9 us; the launch traced here: 23.7 us
  Pallas kernels  23.1 us (97%)
  between operations  0.64 us (3%)
    pallas_call x1, Pallas kernels, on_device(): pl.pallas_call(functools.partial(kernel, inner_size, outer_size), out_sha...  22.2 us
    pallas_call x1, Pallas kernels, on_device(): pl.pallas_call(write_out, out_shape=tuple((jax.ShapeDtypeStruct((1,) + re...  0.85 us

commit v1 on v0

--- a/solution.py
+++ b/solution.py
@@ -12,7 +12,6 @@
 VMEM_BYTES = 48 * 1024 * 1024
 MESH = pl.DeviceIdType.MESH
 HEADS_PER_STEP = 8
-GREET = (1, -1, 2, -2)
 CONTRACT_LAST = (((1,), (1,)), ((), ()))
 
 
@@ -28,7 +27,7 @@
     inner_size, outer_size,
     q_ref, k_ref, v_ref, g_ref, start_ref,
     dq_ref, dk_ref, dv_ref,
-    qs, gs, ks, vs, kt, bias, early, prob, plow, ds, start_rows, own_sum, part, came,
+    qs, gs, ks, vs, kt, bias, early, stat, prob, plow, ds, start_rows, own_sum, part, came,
     local_sem, send_sem, recv_sem,
 ):
     length = k_ref.shape[1]
@@ -36,15 +35,25 @@
     heads = q_ref.shape[2] // size
     scale = size ** (-0.5)
     blocks = inner_size * outer_size
-    block = lax.axis_index("inner") * outer_size + lax.axis_index("outer")
+    outer = lax.axis_index("outer")
+    block = lax.axis_index("inner") * outer_size + outer
 
     def at(step):
         other = lax.rem(block + step + blocks, blocks)
         return (other // outer_size, lax.rem(other, outer_size))
 
+    opens = outer == 0
+    skips = jnp.logical_and(outer == outer_size - 2, block + 2 < blocks)
+    passes = jnp.logical_and(outer < outer_size - 1, block >= 1)
+    has_next = block + 1 < blocks
+
     barrier = pltpu.get_barrier_semaphore()
-    for step in GREET:
+
+    def greet(step):
         pl.semaphore_signal(barrier, inc=1, device_id=at(step), device_id_type=MESH)
+
+    pl.when(block >= 1)(lambda: greet(-1))
+    pl.when(jnp.logical_and(opens, block >= 2))(lambda: greet(-2))
 
     loads = []
 
@@ -60,22 +69,43 @@
         load(q_ref.at[0, :, pl.ds(head * size, size)], qs.at[pl.ds(head * length, length)])
         load(g_ref.at[0, :, pl.ds(head * size, size)], gs.at[pl.ds(head * length, length)])
 
-    pl.semaphore_wait(barrier, len(GREET))
+    own_rows, near_rows, far_rows = (pl.ds(tile * length, length) for tile in range(3))
+
+    greeters = has_next.astype(jnp.int32) + skips.astype(jnp.int32)
+    pl.when(has_next)(lambda: pl.semaphore_wait(barrier, greeters))
     sends = []
 
-    def send(source, target, step):
-        which = len(sends)
-        copy = pltpu.make_async_remote_copy(
+    def remote(source, target, step, give, take):
+        return pltpu.make_async_remote_copy(
             src_ref=source, dst_ref=target,
-            send_sem=send_sem.at[which], recv_sem=recv_sem.at[which],
+            send_sem=send_sem.at[give], recv_sem=recv_sem.at[take],
             device_id=at(step), device_id_type=MESH,
         )
-        copy.start()
-        sends.append(copy)
+
+    def send(cond, *args):
+        copy = remote(*args)
+        pl.when(cond)(copy.start)
+        sends.append((cond, copy))
         return copy
 
-    key_near = send(k_ref.at[0], ks.at[pl.ds(length, length)], 1)
-    value_near = send(v_ref.at[0], vs.at[pl.ds(length, length)], 1)
+    key_near = send(has_next, k_ref.at[0], ks.at[near_rows], 1, 0, 0)
+    key_far = send(skips, k_ref.at[0], ks.at[far_rows], 2, 2, 2)
+    value_near = send(has_next, v_ref.at[0], vs.at[near_rows], 1, 1, 1)
+    value_far = send(skips, v_ref.at[0], vs.at[far_rows], 2, 3, 3)
+
+    def blank(rows):
+        ks[rows] = jnp.zeros((length, size), jnp.bfloat16)
+        vs[rows] = jnp.zeros((length, size), jnp.bfloat16)
+
+    pl.when(block < 1)(lambda: blank(near_rows))
+    pl.when(block < 2)(lambda: blank(far_rows))
+
+    def no_part(slot):
+        came[slot] = jnp.zeros((length, size), jnp.bfloat16)
+
+    for tile in (1, 2):
+        for kind in range(2):
+            pl.when(block + tile >= blocks)(functools.partial(no_part, 2 * kind + tile - 1))
 
     first = block * length
     key_at = lax.broadcasted_iota(jnp.int32, (length, length), 0)
@@ -124,56 +154,65 @@
     def rows_of(head):
         return pl.ds(pl.multiple_of(head * length, length), length)
 
-    own_rows, near_rows, far_rows = (pl.ds(tile * length, length) for tile in range(3))
-
     def own_tile(head):
         early[0, head] = dot_last(ks[own_rows], qs[rows_of(head)]) + bias[own_rows]
         early[2, head] = dot_last(vs[own_rows], gs[rows_of(head)])
 
     def near_scores(head):
-        early[1, head] = dot_last(ks[near_rows], qs[rows_of(head)]) + bias[near_rows]
+        scores = dot_last(ks[near_rows], qs[rows_of(head)]) + bias[near_rows]
+        top = jnp.max(scores, axis=0, keepdims=True)
+        weights = jnp.exp2((scores - top) * (scale * LOG2E))
+        early[1, head] = weights
+        stat[head, 0:1] = top
+        stat[head, 1:2] = jnp.sum(weights, axis=0, keepdims=True)
 
     def near_grads(head):
         early[3, head] = dot_last(vs[near_rows], gs[rows_of(head)])
 
     over_heads(own_tile)
-    key_near.wait_recv()
-    key_far = send(ks.at[near_rows], ks.at[far_rows], 1)
+    pl.when(block >= 1)(key_near.wait_recv)
+    send(passes, ks.at[near_rows], ks.at[far_rows], 1, 4, 2)
     over_heads(near_scores)
-    value_near.wait_recv()
-    value_far = send(vs.at[near_rows], vs.at[far_rows], 1)
+    pl.when(block >= 1)(value_near.wait_recv)
+    send(passes, vs.at[near_rows], vs.at[far_rows], 1, 5, 3)
     over_heads(near_grads)
-    key_far.wait_recv()
+    pl.when(block >= 2)(key_far.wait_recv)
 
     def forward(head):
         far = dot_last(ks[far_rows], qs[rows_of(head)]) + bias[own_rows]
         mixed = merge(early[0, head], far)
-        near = early[1, head]
-        top = jnp.maximum(
-            jnp.max(mixed, axis=0, keepdims=True), jnp.max(near, axis=0, keepdims=True)
-        )
+        near_top = stat[head, 0:1]
+        top = jnp.maximum(jnp.max(mixed, axis=0, keepdims=True), near_top)
         mixed = jnp.exp2((mixed - top) * (scale * LOG2E))
-        near = jnp.exp2((near - top) * (scale * LOG2E))
-        total = jnp.sum(mixed, axis=0, keepdims=True) + jnp.sum(near, axis=0, keepdims=True)
+        shrink = jnp.exp2((near_top - top) * (scale * LOG2E))
+        total = jnp.sum(mixed, axis=0, keepdims=True) + shrink * stat[head, 1:2]
         inverse = 1.0 / total
         mixed = mixed * inverse
-        near = near * inverse
+        near = early[1, head] * (shrink * inverse)
         prob[head, pl.ds(0, length)] = mixed
         prob[head, pl.ds(length, length)] = near
         put(plow, head, mixed, near)
 
     over_heads(forward)
 
+    lead = jnp.where(opens, 1, 2)
+
+    def back(kind, tile):
+        slot = 2 * kind + tile - 1
+        return remote(part.at[slot], came.at[slot], -tile, 6 + slot, 4 + slot)
+
     def give_back(weights, rows, kind):
-        copies = []
-        for tile in (2, 1):
-            slot = 2 * kind + tile - 1
-            part[slot] = dot(weights[pl.ds(tile * length, length)], rows[...]).astype(jnp.bfloat16)
-            copies.append(send(part.at[slot], came.at[slot], -tile))
-        return copies
-
-    value_parts = give_back(plow, gs, 0)
-    value_far.wait_recv()
+        for tile in (lead, 3 - lead):
+            from_rows = pl.ds(pl.multiple_of(tile * length, length), length)
+            part[2 * kind + tile - 1] = dot(weights[from_rows], rows[...]).astype(jnp.bfloat16)
+            pl.when(block >= tile)(back(kind, tile).start)
+
+    def take_back(kind):
+        for tile in (1, 2):
+            pl.when(block + tile < blocks)(back(kind, tile).wait_recv)
+
+    give_back(plow, gs, 0)
+    pl.when(block >= 2)(value_far.wait_recv)
 
     def backward(head):
         mixed = merge(early[2, head], dot_last(vs[far_rows], gs[rows_of(head)]))
@@ -186,7 +225,7 @@
         put(ds, head, mixed_prob * (mixed - delta), near_prob * (near - delta))
 
     over_heads(backward)
-    key_parts = give_back(ds, qs, 1)
+    give_back(ds, qs, 1)
 
     own_sum[0] = dot(plow[own_rows], gs[...])
     own_sum[1] = dot(ds[own_rows], qs[...])
@@ -196,18 +235,19 @@
         turned = dot(kt[...], ds[:, pl.ds(head * length, length)]) * scale
         dq_ref[:, pl.ds(head * size, size)] = turned.T.astype(jnp.bfloat16)
 
-    for copy in value_parts:
-        copy.wait_recv()
+    take_back(0)
     dv_ref[...] = (
         own_sum[0] + came[0].astype(jnp.float32) + came[1].astype(jnp.float32)
     ).astype(jnp.bfloat16)
-    for copy in key_parts:
-        copy.wait_recv()
+    take_back(1)
     dk_ref[...] = (
         (own_sum[1] + came[2].astype(jnp.float32) + came[3].astype(jnp.float32)) * scale
     ).astype(jnp.bfloat16)
-    for copy in sends:
-        copy.wait_send()
+    for cond, copy in sends:
+        pl.when(cond)(copy.wait_send)
+    for kind in range(2):
+        for tile in (1, 2):
+            pl.when(block >= tile)(back(kind, tile).wait_send)
 
 
 def write_out(dq_from, dk_from, dv_from, dq_ref, dk_ref, dv_ref, sem):
@@ -246,6 +286,7 @@
             pltpu.VMEM((size, 3 * length), low),
             pltpu.VMEM((2 * length, length), wide),
             pltpu.VMEM((4, heads, length, length), wide),
+            pltpu.VMEM((heads, 8, length), wide),
             pltpu.VMEM((heads, 2 * length, length), wide),
             pltpu.VMEM((3 * length, heads * length), low),
             pltpu.VMEM((3 * length, heads * length), low),
@@ -254,7 +295,7 @@
             pltpu.VMEM((4, length, size), low),
             pltpu.VMEM((4, length, size), low),
             pltpu.SemaphoreType.DMA((3 + 2 * heads,)),
-            pltpu.SemaphoreType.DMA((8,)),
+            pltpu.SemaphoreType.DMA((10,)),
             pltpu.SemaphoreType.DMA((8,)),
         ],
         compiler_params=pltpu.CompilerParams(

time: 23.9 us -> 23.6 us (0.987)
  the two profiles are of different devices: /device:TPU:0 before, /device:TPU:27 now
where the time goes in v1:
time: 23.6 us; the launch traced here: 23.4 us
  Pallas kernels  22.8 us (97%)
  between operations  0.64 us (3%)
    pallas_call x1, Pallas kernels, on_device(): pl.pallas_call(functools.partial(kernel, inner_size, outer_size), out_sha...  21.9 us
    pallas_call x1, Pallas kernels, on_device(): pl.pallas_call(write_out, out_shape=tuple((jax.ShapeDtypeStruct((1,) + re...  0.85 us

profile of v1, /device:TPU:27, one launch (start us, length us, event | category | flops | bytes accessed | tf_op | source)
XLA Modules:
  0.0 23.4 jit_solution(18291105536337845266)
XLA Ops:
  0.6 21.9 %window_attention_grad.1 = (bf16[256,1024]{1,0:T(8,128)(2,1)S(1)}, bf16[256,128]{1,0:T(8,128)(2,1)S(1)}, bf16[256,128]{1,0:T(8,128)(2,1)S(1)}) custom-call(bf16[1,256,1024]{2,1,0:T(8,128)(2,1)} %q_ref.1, bf16[1,256,128]{2,1,0:T(8,128)(2,1)} %k_ref.1, bf16[1,256,128]{2,1,0:T(8,128)(2,1)} %v_ref.1, bf16[1,256,1024]{2,1,0:T(8,128)(2,1)} %g_ref.1, ...), custom_call_target="tpu_custom_call" | custom-call | tf_op jit(solution)/shard_map/window_attention_grad/pallas_call | solution.py:272
  22.6 0.9 %write_out.1 = (bf16[1,256,1024]{2,1,0:T(8,128)(2,1)}, bf16[1,256,128]{2,1,0:T(8,128)(2,1)}, bf16[1,256,128]{2,1,0:T(8,128)(2,1)}) custom-call(bf16[256,1024]{1,0:T(8,128)(2,1)S(1)} %get-tuple-element.6.dq_from, bf16[256,128]{1,0:T(8,128)(2,1)S(1)} %get-tuple-element.7.dk_from, bf16[256,128]{1,0:T(8,128)(2,1)S(1)} %get-tuple-element.8.dv_from), custom_call_target="tpu_custom_call" | custom-call | tf_op jit(solution)/shard_map/write_out/pallas_call | solution.py:306

commit v2 on v1

--- a/solution.py
+++ b/solution.py
@@ -11,6 +11,7 @@
 LOG2E = 1.4426950408889634
 VMEM_BYTES = 48 * 1024 * 1024
 MESH = pl.DeviceIdType.MESH
+CHAINED = (1,)
 HEADS_PER_STEP = 8
 CONTRACT_LAST = (((1,), (1,)), ((), ()))
 
@@ -27,7 +28,7 @@
     inner_size, outer_size,
     q_ref, k_ref, v_ref, g_ref, start_ref,
     dq_ref, dk_ref, dv_ref,
-    qs, gs, ks, vs, kt, bias, early, stat, prob, plow, ds, start_rows, own_sum, part, came,
+    qs, gs, ks, vs, kt, bias, early, stat, own_mask, prob, plow, ds, start_rows, own_sum, part, came,
     local_sem, send_sem, recv_sem,
 ):
     length = k_ref.shape[1]
@@ -103,9 +104,18 @@
     def no_part(slot):
         came[slot] = jnp.zeros((length, size), jnp.bfloat16)
 
+    second, last = outer == 1, outer == outer_size - 1
+
+    def expects(kind, tile):
+        there = block + tile < blocks
+        if kind not in CHAINED:
+            return there
+        return jnp.logical_and(there, jnp.logical_not(last if tile == 1 else second))
+
     for tile in (1, 2):
         for kind in range(2):
-            pl.when(block + tile >= blocks)(functools.partial(no_part, 2 * kind + tile - 1))
+            missing = jnp.logical_not(expects(kind, tile))
+            pl.when(missing)(functools.partial(no_part, 2 * kind + tile - 1))
 
     first = block * length
     key_at = lax.broadcasted_iota(jnp.int32, (length, length), 0)
@@ -120,15 +130,12 @@
     for copy in loads[1:]:
         copy.wait()
 
+    own_mask[...] = jnp.where(causal, 1.0, 0.0).astype(jnp.bfloat16)
+
     def split(mixed):
-        is_own = lax.broadcasted_iota(jnp.int32, (length, length), 0) <= lax.broadcasted_iota(
-            jnp.int32, (length, length), 1
-        )
-        zero = jnp.zeros_like(mixed)
-        return (
-            jnp.where(is_own, mixed, zero).astype(jnp.bfloat16),
-            jnp.where(is_own, zero, mixed).astype(jnp.bfloat16),
-        )
+        low = mixed.astype(jnp.bfloat16)
+        own = low * own_mask[...]
+        return own, low - own
 
     def merge(own, far):
         is_own = lax.broadcasted_iota(jnp.int32, (length, length), 0) <= lax.broadcasted_iota(
@@ -195,21 +202,45 @@
 
     over_heads(forward)
 
-    lead = jnp.where(opens, 1, 2)
-
-    def back(kind, tile):
+    gathers = jnp.where(second, 2, jnp.where(outer == outer_size - 2, 1, 0))
+
+    def back(kind, tile, to_slot=None, step=None):
         slot = 2 * kind + tile - 1
-        return remote(part.at[slot], came.at[slot], -tile, 6 + slot, 4 + slot)
+        to_slot = slot if to_slot is None else to_slot
+        step = -tile if step is None else step
+        return remote(part.at[slot], came.at[to_slot], step, 6 + slot, 4 + to_slot)
 
     def give_back(weights, rows, kind):
+        chained = kind in CHAINED
+        lead = jnp.where(outer < 2, 1, 2) if chained else jnp.where(opens, 1, 2)
         for tile in (lead, 3 - lead):
+            slot = 2 * kind + tile - 1
             from_rows = pl.ds(pl.multiple_of(tile * length, length), length)
-            part[2 * kind + tile - 1] = dot(weights[from_rows], rows[...]).astype(jnp.bfloat16)
-            pl.when(block >= tile)(back(kind, tile).start)
+            part[slot] = dot(weights[from_rows], rows[...]).astype(jnp.bfloat16)
+            ready = block >= tile
+            if not chained:
+                pl.when(ready)(back(kind, tile).start)
+                continue
+            up = jnp.logical_and(opens, tile == 1)
+            down = jnp.logical_and(last, tile == 2)
+            aside = jnp.logical_or(up, down)
+            step = jnp.where(aside, jnp.where(up, 1, -1), -tile)
+            to_slot = jnp.where(aside, 4 + kind, slot)
+            pl.when(jnp.logical_and(ready, tile != gathers))(back(kind, tile, to_slot, step).start)
+
+    def settle(kind):
+        slot = jnp.maximum(2 * kind + gathers - 1, 0)
+
+        @pl.when(jnp.logical_and(gathers > 0, block >= gathers))
+        def _():
+            back(kind, 1, 4 + kind).wait_recv()
+            both = part[slot].astype(jnp.float32) + came[4 + kind].astype(jnp.float32)
+            part[slot] = both.astype(jnp.bfloat16)
+            remote(part.at[slot], came.at[slot], -gathers, 6 + slot, 4 + slot).start()
 
     def take_back(kind):
         for tile in (1, 2):
-            pl.when(block + tile < blocks)(back(kind, tile).wait_recv)
+            pl.when(expects(kind, tile))(back(kind, tile).wait_recv)
 
     give_back(plow, gs, 0)
     pl.when(block >= 2)(value_far.wait_recv)
@@ -229,6 +260,7 @@
 
     own_sum[0] = dot(plow[own_rows], gs[...])
     own_sum[1] = dot(ds[own_rows], qs[...])
+    settle(1)
     kt[...] = ks[...].astype(jnp.float32).T.astype(jnp.bfloat16)
 
     for head in range(heads):
@@ -287,16 +319,17 @@
             pltpu.VMEM((2 * length, length), wide),
             pltpu.VMEM((4, heads, length, length), wide),
             pltpu.VMEM((heads, 8, length), wide),
+            pltpu.VMEM((length, length), low),
             pltpu.VMEM((heads, 2 * length, length), wide),
             pltpu.VMEM((3 * length, heads * length), low),
             pltpu.VMEM((3 * length, heads * length), low),
             pltpu.VMEM((1, length), jnp.int32),
             pltpu.VMEM((2, length, size), wide),
             pltpu.VMEM((4, length, size), low),
-            pltpu.VMEM((4, length, size), low),
+            pltpu.VMEM((6, length, size), low),
             pltpu.SemaphoreType.DMA((3 + 2 * heads,)),
             pltpu.SemaphoreType.DMA((10,)),
-            pltpu.SemaphoreType.DMA((8,)),
+            pltpu.SemaphoreType.DMA((10,)),
         ],
         compiler_params=pltpu.CompilerParams(
             collective_id=0, has_side_effects=True, vmem_limit_bytes=VMEM_BYTES

time: 23.6 us -> 23.3 us (0.987)
  Pallas kernels: 22.8 us -> 22.5 us
    pallas_call x1, Pallas kernels: 21.9 us -> 21.6 us  [on_device(): pl.pallas_call(functools.partial(kernel, inner_size, outer_size), out_sha...]
where the time goes in v2:
time: 23.3 us; the launch traced here: 23.1 us
  Pallas kernels  22.5 us (97%)
  between operations  0.64 us (3%)
    pallas_call x1, Pallas kernels, on_device(): pl.pallas_call(functools.partial(kernel, inner_size, outer_size), out_sha...  21.6 us
    pallas_call x1, Pallas kernels, on_device(): pl.pallas_call(write_out, out_shape=tuple((jax.ShapeDtypeStruct((1,) + re...  0.85 us

profile of v2, /device:TPU:27, one launch (start us, length us, event | category | flops | bytes accessed | tf_op | source)
XLA Modules:
  0.0 23.1 jit_solution(7139532790075337657)
XLA Ops:
  0.6 21.6 %window_attention_grad.1 = (bf16[256,1024]{1,0:T(8,128)(2,1)S(1)}, bf16[256,128]{1,0:T(8,128)(2,1)S(1)}, bf16[256,128]{1,0:T(8,128)(2,1)S(1)}) custom-call(bf16[1,256,1024]{2,1,0:T(8,128)(2,1)} %q_ref.1, bf16[1,256,128]{2,1,0:T(8,128)(2,1)} %k_ref.1, bf16[1,256,128]{2,1,0:T(8,128)(2,1)} %v_ref.1, bf16[1,256,1024]{2,1,0:T(8,128)(2,1)} %g_ref.1, ...), custom_call_target="tpu_custom_call" | custom-call | tf_op jit(solution)/shard_map/window_attention_grad/pallas_call | solution.py:304
  22.3 0.9 %write_out.1 = (bf16[1,256,1024]{2,1,0:T(8,128)(2,1)}, bf16[1,256,128]{2,1,0:T(8,128)(2,1)}, bf16[1,256,128]{2,1,0:T(8,128)(2,1)}) custom-call(bf16[256,1024]{1,0:T(8,128)(2,1)S(1)} %get-tuple-element.6.dq_from, bf16[256,128]{1,0:T(8,128)(2,1)S(1)} %get-tuple-element.7.dk_from, bf16[256,128]{1,0:T(8,128)(2,1)S(1)} %get-tuple-element.8.dv_from), custom_call_target="tpu_custom_call" | custom-call | tf_op jit(solution)/shard_map/write_out/pallas_call | solution.py:339
